TPU v7x, 32 devices: a whole 2x2x4 slice. The times are simulated.
32 devices in a mesh: scan: 2 (over x), tile: 16 (over z, y, core).
Axes of the slice: x: 2, y: 2, z: 4, core: 2. Of those that a mesh axis runs over, the one named last changes fastest.
Arguments:
- slices: float32 [4, 2, 1024, 1024], P(None, None, ('scan', 'tile')), parts along dimension 2, may hold values from -4 to 4
- probe_modes: float32 [4, 2, 128, 128], P('scan'), parts along dimension 0, may hold values from -4 to 4
- row_offset: int32 [128], P(('scan', 'tile')), parts along dimension 0, may hold values from 0 to 31, as said below
- col_offset: int32 [128], P(('scan', 'tile')), parts along dimension 0, may hold values from 0 to 1023
- amplitude: float32 [128, 128, 128], P(('scan', 'tile')), parts along dimension 0, may hold values from 0.5 to 3
Outputs:
- slice_grad: float32 [4, 2, 1024, 1024], P(None, None, ('scan', 'tile')), parts along dimension 2
- probe_grad: float32 [4, 2, 128, 128], P('scan'), parts along dimension 0
There are 2 independent parts, one for each index of `scan`. A program takes and returns all parts, laid end to end along the dimension named above; each array names one. Nothing has to cross between parts.
Inputs may be any that keep to these rules, and one draw needn't show every extreme that they name: Window w starts 32 * (w // 4) + row_offset[w] rows down the object; the largest value is taken by some window in every draw.
All inputs are finite; a program needn't handle non-finite values.
Results may differ from a plain program's by a relative error of at most 0.0003.
Values sent between devices are 32-bit elements; how exact they have to be, the bound alone decides.
A program may use at most 128 MiB of HBM per device.

v0:
```python
import math
import jax
import jax.numpy as jnp
from jax import lax
from jax.sharding import PartitionSpec as P

INTENSITY_SHIFT = 0.5
FRESNEL = 0.75


def from_behind(value, axis, steps):
    count = lax.axis_size(axis)
    pairs = [(source, (source + steps) % count) for source in range(count)]
    return lax.ppermute(value, axis, pairs)


def dft_tables(window_side):
    steps_idx = jnp.arange(window_side, dtype=jnp.int32)
    product = steps_idx[:, None] * steps_idx[None, :] % window_side
    angles = product.astype(jnp.float32) * (-2.0 * math.pi / window_side)
    scale = 1.0 / math.sqrt(window_side)
    return (jnp.cos(angles) * scale, jnp.sin(angles) * scale)


def fresnel_kernel(window_side):
    steps_idx = jnp.arange(window_side, dtype=jnp.int32)
    freqs = (steps_idx + window_side // 2) % window_side - window_side // 2
    radius = (freqs[:, None] * freqs[:, None] + freqs[None, :] * freqs[None, :]).astype(jnp.float32)
    phase = radius * (-math.pi * FRESNEL / (window_side / 2.0) ** 2)
    return (jnp.cos(phase), jnp.sin(phase))


def left_apply(mat_real, mat_imag, wave_real, wave_imag):

    def product(matrix, field):
        return jnp.einsum("jk,mkl->mjl", matrix, field, precision=lax.Precision.HIGHEST)

    return (
        product(mat_real, wave_real) - product(mat_imag, wave_imag),
        product(mat_real, wave_imag) + product(mat_imag, wave_real),
    )


def right_apply(wave_real, wave_imag, mat_real, mat_imag):

    def product(field, matrix):
        return jnp.einsum("mjk,kl->mjl", field, matrix, precision=lax.Precision.HIGHEST)

    return (
        product(wave_real, mat_real) - product(wave_imag, mat_imag),
        product(wave_imag, mat_real) + product(wave_real, mat_imag),
    )


def transform(wave_real, wave_imag, mat_real, mat_imag):
    half_real, half_imag = left_apply(mat_real, mat_imag, wave_real, wave_imag)
    return right_apply(half_real, half_imag, mat_real, mat_imag)


def propagate(wave_real, wave_imag, tables):
    cos_table, sin_table, kernel_real, kernel_imag = tables
    spec_real, spec_imag = transform(wave_real, wave_imag, cos_table, sin_table)
    moved_real = spec_real * kernel_real - spec_imag * kernel_imag
    moved_imag = spec_real * kernel_imag + spec_imag * kernel_real
    return transform(moved_real, moved_imag, cos_table, -sin_table)


def window_loss(crops, probe_modes, measured, tables):
    cos_table, sin_table = (tables[0], tables[1])
    wave_real = probe_modes[:, 0]
    wave_imag = probe_modes[:, 1]
    slice_count = crops.shape[0]
    exit_real = wave_real
    exit_imag = wave_imag
    for depth_index in range(slice_count):
        trans_real = crops[depth_index, 0]
        trans_imag = crops[depth_index, 1]
        exit_real = trans_real * wave_real - trans_imag * wave_imag
        exit_imag = trans_real * wave_imag + trans_imag * wave_real
        if depth_index + 1 < slice_count:
            wave_real, wave_imag = propagate(exit_real, exit_imag, tables)
    far_real, far_imag = transform(exit_real, exit_imag, cos_table, sin_table)
    intensity = jnp.sum(far_real * far_real + far_imag * far_imag, axis=0)
    modelled = jnp.sqrt(intensity + INTENSITY_SHIFT)
    return 0.5 * jnp.sum((modelled - measured) ** 2)


def window_grads(crops, probe_modes, measured, tables):
    return jax.grad(window_loss, argnums=(0, 1))(crops, probe_modes, measured, tables)


def on_device(slices, probe_modes, row_offset, col_offset, amplitude):
    window_side = probe_modes.shape[-1]
    slice_count = slices.shape[0]
    rows_here = slices.shape[2]
    cols_here = slices.shape[3]
    upper_count = (window_side - 2) // rows_here + 1
    cos_table, sin_table = dft_tables(window_side)
    kernel_real, kernel_imag = fresnel_kernel(window_side)
    tables = (cos_table, sin_table, kernel_real, kernel_imag)
    pieces = [slices]
    moving = slices
    for offset in range(upper_count):
        moving = from_behind(moving, "tile", -1)
        pieces.append(moving)
    extended = jnp.concatenate(pieces, axis=2)[:, :, : rows_here + window_side - 1]
    extended = jnp.concatenate([extended, extended[:, :, :, : window_side - 1]], axis=3)
    anchor = jnp.zeros((), jnp.int32)
    crop_shape = (slice_count, 2, window_side, window_side)

    def one_window(row_start, col_start, measured):
        corner = (anchor, anchor, row_start, col_start)
        crops = lax.dynamic_slice(extended, corner, crop_shape)
        return window_grads(crops, probe_modes, measured, tables)

    crop_grads, probe_terms = jax.vmap(one_window)(row_offset, col_offset, amplitude)

    def add_window(window_index, gradient_buffer):
        corner = (anchor, anchor, row_offset[window_index], col_offset[window_index])
        current = lax.dynamic_slice(gradient_buffer, corner, crop_shape)
        return lax.dynamic_update_slice(gradient_buffer, current + crop_grads[window_index], corner)

    gradient_buffer = lax.fori_loop(
        0, row_offset.shape[0], add_window, jnp.zeros(extended.shape, jnp.float32)
    )
    folded = (
        gradient_buffer[:, :, :, :cols_here]
        .at[:, :, :, : window_side - 1]
        .add(gradient_buffer[:, :, :, cols_here:])
    )
    pad_rows = (upper_count + 1) * rows_here - folded.shape[2]
    padded = jnp.pad(folded, ((0, 0), (0, 0), (0, pad_rows), (0, 0)))
    shares = [
        padded[:, :, offset * rows_here : (offset + 1) * rows_here]
        for offset in range(upper_count + 1)
    ]
    own_grad = shares[0]
    for offset in range(1, upper_count + 1):
        own_grad = own_grad + from_behind(shares[offset], "tile", offset)
    probe_grad = lax.psum(jnp.sum(probe_terms, axis=0), "tile")
    return (own_grad, probe_grad)


def solution(mesh):
    placed = (
        P(None, None, ("scan", "tile"), None),
        P("scan", None, None, None),
        P(("scan", "tile")),
        P(("scan", "tile")),
        P(("scan", "tile"), None, None),
    )
    return jax.shard_map(
        on_device,
        mesh=mesh,
        in_specs=placed,
        out_specs=(P(None, None, ("scan", "tile"), None), P("scan", None, None, None)),
        check_vma=False,
    )
```

profile of v0, /device:TPU:0, one launch (start us, length us, event | category | flops | bytes accessed | tf_op | source)
XLA Modules:
  0.0 459.7 jit_solution(3375297501975912838)
XLA Ops:
  7.2 5.5 %collective-permute-start = (f32[4,2,32,1024]{3,2,1,0:T(8,128)}, f32[4,2,32,1024]{3,2,1,0:T(8,128)S(1)}, u32[]{:S(2)}, u32[]{:S(2)}) collective-permute-start(f32[4,2,32,1024]{3,2,1,0:T(8,128)} %param.9), channel_id=1, source_target_pairs={{0,15},{1,0},{2,1},{3,2},{4,3},{5,4},{6,5},{7,6},{8,7},{9,8},{10,9... | collective-permute-start | bytes 3145736 | tf_op jit(solution)/shard_map/ppermute | solution.py:14
  12.7 12.6 %collective-permute-done = f32[4,2,32,1024]{3,2,1,0:T(8,128)S(1)} collective-permute-done((f32[4,2,32,1024]{3,2,1,0:T(8,128)}, f32[4,2,32,1024]{3,2,1,0:T(8,128)S(1)}, u32[]{:S(2)}, u32[]{:S(2)}) %collective-permute-start) | collective-permute-done | bytes 1048608 | tf_op jit(solution)/shard_map/ppermute | solution.py:14
  25.4 4.5 collective-permute-start.1
  29.9 12.3 %collective-permute-done.1 = f32[4,2,32,1024]{3,2,1,0:T(8,128)S(1)} collective-permute-done((f32[4,2,32,1024]{3,2,1,0:T(8,128)S(1)}, f32[4,2,32,1024]{3,2,1,0:T(8,128)S(1)}, u32[]{:S(2)}, u32[]{:S(2)}) %collective-permute-start.1) | collective-permute-done | bytes 1048608 | tf_op jit(solution)/shard_map/ppermute | solution.py:14
  42.2 4.6 %collective-permute-start.2 = (f32[4,2,32,1024]{3,2,1,0:T(8,128)S(1)}, f32[4,2,32,1024]{3,2,1,0:T(8,128)S(1)}, u32[]{:S(2)}, u32[]{:S(2)}) collective-permute-start(f32[4,2,32,1024]{3,2,1,0:T(8,128)S(1)} %collective-permute-done.1), channel_id=1, source_target_pairs={{0,15},{1,0},{2,1},{3,2},{4,3},{5,4},{6,5},{7,6},{8,7},{9,8},{10,9... | collective-permute-start | bytes 3145736 | tf_op jit(solution)/shard_map/ppermute | solution.py:14
  49.1 10.0 %collective-permute-done.2 = f32[4,2,32,1024]{3,2,1,0:T(8,128)S(1)} collective-permute-done((f32[4,2,32,1024]{3,2,1,0:T(8,128)S(1)}, f32[4,2,32,1024]{3,2,1,0:T(8,128)S(1)}, u32[]{:S(2)}, u32[]{:S(2)}) %collective-permute-start.2) | collective-permute-done | bytes 1048608 | tf_op jit(solution)/shard_map/ppermute | solution.py:14
  59.1 4.6 %collective-permute-start.3 = (f32[4,2,32,1024]{3,2,1,0:T(8,128)S(1)}, f32[4,2,32,1024]{3,2,1,0:T(8,128)}, u32[]{:S(2)}, u32[]{:S(2)}) collective-permute-start(f32[4,2,32,1024]{3,2,1,0:T(8,128)S(1)} %collective-permute-done.2), channel_id=1, source_target_pairs={{0,15},{1,0},{2,1},{3,2},{4,3},{5,4},{6,5},{7,6},{8,7},{9,8},{10,9... | collective-permute-start | bytes 3145736 | tf_op jit(solution)/shard_map/ppermute | solution.py:14
  64.6 1.3 constant_dynamic-update-slice_fusion.4
  67.2 8.8 %collective-permute-done.3 = f32[4,2,32,1024]{3,2,1,0:T(8,128)} collective-permute-done((f32[4,2,32,1024]{3,2,1,0:T(8,128)S(1)}, f32[4,2,32,1024]{3,2,1,0:T(8,128)}, u32[]{:S(2)}, u32[]{:S(2)}) %collective-permute-start.3) | collective-permute-done | bytes 1048608 | tf_op jit(solution)/shard_map/ppermute | solution.py:14
  76.0 1.3 constant_dynamic-update-slice_fusion
  77.4 3.2 pad_maximum_fusion
  80.6 17.3 %while.16 = (s32[]{:T(128)}, f32[4,2,159,1151]{3,2,1,0:T(8,128)}, s32[4,4]{1,0:T(4,128)S(1)}, f32[4,4,2,128,128]{4,3,2,1,0:T(8,128)}, s32[]{:T(128)}) while((s32[]{:T(128)}, f32[4,2,159,1151]{3,2,1,0:T(8,128)}, s32[4,4]{1,0:T(4,128)S(1)}, f32[4,4,2,128,128]{4,3,2,1,0:T(8,128)}, s32[]{:T(128)}) %tuple.92), condition=%wide.while_cond.1, body=%wide.while_body.1.sunk | while | flops 2 | bytes 1050225 | solution.py:113
  81.3 3.6 bitcast_dynamic-update-slice_fusion.2
  85.5 3.6 bitcast_dynamic-update-slice_fusion.2
  89.8 3.6 bitcast_dynamic-update-slice_fusion.2
  94.1 3.6 bitcast_dynamic-update-slice_fusion.2
  97.9 1.7 slice_bitcast_fusion.7
  107.7 1.2 fusion.84
  108.9 1.2 fusion.83
  110.1 1.4 fusion.38
  112.7 1.2 fusion.39
  117.4 1.2 fusion.236
  118.6 1.2 fusion.232
  119.7 1.2 fusion.37
  122.1 1.6 fusion.36
  127.1 1.2 fusion.86
  128.3 1.2 fusion.85
  129.5 1.2 fusion.34
  131.9 1.2 fusion.35
  134.2 1.3 convolution_add_fusion.34
  136.7 1.2 fusion.222
  137.9 1.2 fusion.218
  139.1 1.2 fusion.33
  141.4 1.2 fusion.32
  146.1 1.4 fusion.88
  147.5 1.2 fusion.87
  148.7 1.2 fusion.30
  151.0 1.2 fusion.31
  155.7 1.2 fusion.208
  156.9 1.2 fusion.204
  158.1 1.6 fusion.29
  159.7 1.2 fusion.28
  185.7 1.9 multiply_reduce_fusion.10
  196.2 1.3 fusion.11
  200.9 2.0 multiply_reduce_fusion.6
  216.7 2.2 add_bitcast_fusion.1
  222.3 1.2 add_bitcast_fusion.6
  225.9 3.0 broadcast_in_dim.12
  228.9 54.8 %while.15 = (s32[]{:T(128)}, f32[4,2,159,1151]{3,2,1,0:T(8,128)}, s32[4]{0:T(128)S(1)}, s32[4]{0:T(128)S(1)}, f32[4,4,2,128,128]{4,3,0,2,1:T(8,128)S(1)}, /*index=5*/s32[]{:T(128)}, s32[]{:T(128)}, s32[]{:T(128)}, s32[]{:T(128)}) while((s32[]{:T(128)}, f32[4,2,159,1151]{3,2,1,0:T(8,128)}, s32[4]{0:T(128)S(1)}, s32[4]{0:T(128)S(1)}, ...), condition=%wide.region_18.19_spmd, body=%wide.region_17.18_spmd.sunk | while | flops 131080 | bytes 2621641 | solution.py:123
  233.9 1.5 bitcast_add_fusion.2
  235.4 7.2 %dynamic_update_slice.8 = f32[4,2,159,1151]{3,2,1,0:T(8,128)} dynamic-update-slice(f32[4,2,159,1151]{3,2,1,0:T(8,128)} %get-tuple-element.289, f32[4,2,128,128]{3,2,1,0:T(8,128)S(1)} %bitcast_add_fusion.2, s32[]{:T(128)} %constant.98.clone.1..sunk, s32[]{:T(128)} %constant.98.clone.1..sunk, s32[]{:T(128)S(6)} %select_n.692, s32[]{:T(128)S(6)} %select_n.693) | dynamic-update-slice | bytes 1048580 | tf_op jit(solution)/shard_map/while/body/eval_jaxpr/dynamic_update_slice | solution.py:121
  247.7 1.5 bitcast_add_fusion.2
  249.2 7.0 %dynamic_update_slice.8 = f32[4,2,159,1151]{3,2,1,0:T(8,128)} dynamic-update-slice(f32[4,2,159,1151]{3,2,1,0:T(8,128)} %get-tuple-element.289, f32[4,2,128,128]{3,2,1,0:T(8,128)S(1)} %bitcast_add_fusion.2, s32[]{:T(128)} %constant.98.clone.1..sunk, s32[]{:T(128)} %constant.98.clone.1..sunk, s32[]{:T(128)S(6)} %select_n.692, s32[]{:T(128)S(6)} %select_n.693) | dynamic-update-slice | bytes 1048580 | tf_op jit(solution)/shard_map/while/body/eval_jaxpr/dynamic_update_slice | solution.py:121
  261.3 1.5 bitcast_add_fusion.2
  262.7 7.2 %dynamic_update_slice.8 = f32[4,2,159,1151]{3,2,1,0:T(8,128)} dynamic-update-slice(f32[4,2,159,1151]{3,2,1,0:T(8,128)} %get-tuple-element.289, f32[4,2,128,128]{3,2,1,0:T(8,128)S(1)} %bitcast_add_fusion.2, s32[]{:T(128)} %constant.98.clone.1..sunk, s32[]{:T(128)} %constant.98.clone.1..sunk, s32[]{:T(128)S(6)} %select_n.692, s32[]{:T(128)S(6)} %select_n.693) | dynamic-update-slice | bytes 1048580 | tf_op jit(solution)/shard_map/while/body/eval_jaxpr/dynamic_update_slice | solution.py:121
  275.0 1.5 bitcast_add_fusion.2
  276.5 7.2 %dynamic_update_slice.8 = f32[4,2,159,1151]{3,2,1,0:T(8,128)} dynamic-update-slice(f32[4,2,159,1151]{3,2,1,0:T(8,128)} %get-tuple-element.289, f32[4,2,128,128]{3,2,1,0:T(8,128)S(1)} %bitcast_add_fusion.2, s32[]{:T(128)} %constant.98.clone.1..sunk, s32[]{:T(128)} %constant.98.clone.1..sunk, s32[]{:T(128)S(6)} %select_n.692, s32[]{:T(128)S(6)} %select_n.693) | dynamic-update-slice | bytes 1048580 | tf_op jit(solution)/shard_map/while/body/eval_jaxpr/dynamic_update_slice | solution.py:121
  283.7 5.7 %slice.104 = f32[4,2,159,1024]{3,2,1,0:T(8,128)} slice(f32[4,2,159,1151]{3,2,1,0:T(8,128)} %get-tuple-element.108), slice={[0:4], [0:2], [0:159], [0:1024]} | slice | bytes 10420224 | tf_op jit(solution)/shard_map/slice | solution.py:127
  289.4 1.4 slice_add_fusion.1
  290.8 3.7 scatter-add.4
  294.5 4.1 fusion.846
  299.5 147.3 %all-reduce.13.cloned.1.call-done = f32[2,2,128,128]{2,3,0,1:T(8,128)} async-done(((f32[2,2,128,128]{2,3,0,1:T(8,128)}), f32[2,2,128,128]{2,3,0,1:T(8,128)}) %all-reduce.13.cloned.1.call-update) | async-done | bytes 262160 | tf_op jit(solution)/shard_map/psum | solution.py:140
  446.8 1.8 copy.344
  448.6 4.1 fusion.44
  (158 shorter events, 98.4 us)
Async XLA Ops:
  7.2 439.6 %all-reduce.13.cloned.1.call-start = ((), (), s32[]{:S(2)}) async-start(), calls=%async_computation | async-start | bytes 524288 | tf_op jit(solution)/shard_map/psum | solution.py:140
  7.2 18.2 %collective-permute-start = (f32[4,2,32,1024]{3,2,1,0:T(8,128)}, f32[4,2,32,1024]{3,2,1,0:T(8,128)S(1)}, u32[]{:S(2)}, u32[]{:S(2)}) collective-permute-start(f32[4,2,32,1024]{3,2,1,0:T(8,128)} %param.9), channel_id=1, source_target_pairs={{0,15},{1,0},{2,1},{3,2},{4,3},{5,4},{6,5},{7,6},{8,7},{9,8},{10,9... | collective-permute-start | bytes 3145736 | tf_op jit(solution)/shard_map/ppermute | solution.py:14
  25.4 16.8 %collective-permute-start.1 = (f32[4,2,32,1024]{3,2,1,0:T(8,128)S(1)}, f32[4,2,32,1024]{3,2,1,0:T(8,128)S(1)}, u32[]{:S(2)}, u32[]{:S(2)}) collective-permute-start(f32[4,2,32,1024]{3,2,1,0:T(8,128)S(1)} %collective-permute-done), channel_id=1, source_target_pairs={{0,15},{1,0},{2,1},{3,2},{4,3},{5,4},{6,5},{7,6},{8,7},{9,8},{10,9... | collective-permute-start | bytes 3145736 | tf_op jit(solution)/shard_map/ppermute | solution.py:14
  42.2 16.9 %collective-permute-start.2 = (f32[4,2,32,1024]{3,2,1,0:T(8,128)S(1)}, f32[4,2,32,1024]{3,2,1,0:T(8,128)S(1)}, u32[]{:S(2)}, u32[]{:S(2)}) collective-permute-start(f32[4,2,32,1024]{3,2,1,0:T(8,128)S(1)} %collective-permute-done.1), channel_id=1, source_target_pairs={{0,15},{1,0},{2,1},{3,2},{4,3},{5,4},{6,5},{7,6},{8,7},{9,8},{10,9... | collective-permute-start | bytes 3145736 | tf_op jit(solution)/shard_map/ppermute | solution.py:14
  59.1 16.9 %collective-permute-start.3 = (f32[4,2,32,1024]{3,2,1,0:T(8,128)S(1)}, f32[4,2,32,1024]{3,2,1,0:T(8,128)}, u32[]{:S(2)}, u32[]{:S(2)}) collective-permute-start(f32[4,2,32,1024]{3,2,1,0:T(8,128)S(1)} %collective-permute-done.2), channel_id=1, source_target_pairs={{0,15},{1,0},{2,1},{3,2},{4,3},{5,4},{6,5},{7,6},{8,7},{9,8},{10,9... | collective-permute-start | bytes 3145736 | tf_op jit(solution)/shard_map/ppermute | solution.py:14
  158.1 7.4 %copy-start.7 = (f32[4,128,128]{2,1,0:T(8,128)S(1)}, f32[4,128,128]{2,1,0:T(8,128)}, u32[]{:S(2)}) copy-start(f32[4,128,128]{2,1,0:T(8,128)} %param.13) | copy-start | bytes 786436
  218.9 4.7 %copy-start.1 = (f32[4,128,128]{2,1,0:T(8,128)S(1)}, f32[4,128,128]{2,1,0:T(8,128)}, u32[]{:S(2)}) copy-start(f32[4,128,128]{2,1,0:T(8,128)} %get-tuple-element.139) | copy-start | bytes 786436
  218.9 4.7 %copy-start.2 = (f32[4,128,128]{2,1,0:T(8,128)S(1)}, f32[4,128,128]{2,1,0:T(8,128)}, u32[]{:S(2)}) copy-start(f32[4,128,128]{2,1,0:T(8,128)} %get-tuple-element.140) | copy-start | bytes 786436
  218.9 4.7 %copy-start.3 = (f32[4,128,128]{2,1,0:T(8,128)S(1)}, f32[4,128,128]{2,1,0:T(8,128)}, u32[]{:S(2)}) copy-start(f32[4,128,128]{2,1,0:T(8,128)} %get-tuple-element.141) | copy-start | bytes 786436
  219.7 4.9 %copy-start.4 = (f32[4,128,128]{2,1,0:T(8,128)S(1)}, f32[4,128,128]{2,1,0:T(8,128)}, u32[]{:S(2)}) copy-start(f32[4,128,128]{2,1,0:T(8,128)} %copy.339) | copy-start | bytes 786436
  220.6 4.0 copy-start.5
  221.4 3.2 copy-start.6
  225.6 3.2 copy-start.8
  225.6 3.2 copy-start.9
  294.5 4.2 copy-start
  298.5 150.0 %collective-permute-start.4 = (f32[4,2,32,1024]{3,2,1,0:T(8,128)}, f32[4,2,32,1024]{3,2,1,0:T(8,128)}, u32[]{:S(2)}, u32[]{:S(2)}) collective-permute-start(f32[4,2,32,1024]{3,2,1,0:T(8,128)} %get-tuple-element.169), channel_id=1, source_target_pairs={{0,1},{1,2},{2,3},{3,4},{4,5},{5,6},{6,7},{7,8},{8,9},{9,10},{10,1... | collective-permute-start | bytes 3145736 | tf_op jit(solution)/shard_map/ppermute | solution.py:14
  298.5 150.0 %collective-permute-start.5 = (f32[4,2,32,1024]{3,2,1,0:T(8,128)}, f32[4,2,32,1024]{3,2,1,0:T(8,128)}, u32[]{:S(2)}, u32[]{:S(2)}) collective-permute-start(f32[4,2,32,1024]{3,2,1,0:T(8,128)} %get-tuple-element.172), channel_id=1, source_target_pairs={{0,2},{1,3},{2,4},{3,5},{4,6},{5,7},{6,8},{7,9},{8,10},{9,11},{10,... | collective-permute-start | bytes 3145736 | tf_op jit(solution)/shard_map/ppermute | solution.py:14
  298.5 150.0 %collective-permute-start.6 = (f32[4,2,32,1024]{3,2,1,0:T(8,128)S(1)}, f32[4,2,32,1024]{3,2,1,0:T(8,128)}, u32[]{:S(2)}, u32[]{:S(2)}) collective-permute-start(f32[4,2,32,1024]{3,2,1,0:T(8,128)S(1)} %get-tuple-element.171), channel_id=1, source_target_pairs={{0,3},{1,4},{2,5},{3,6},{4,7},{5,8},{6,9},{7,10},{8,11},{9,12},{10... | collective-permute-start | bytes 3145736 | tf_op jit(solution)/shard_map/ppermute | solution.py:14
  298.6 150.0 %collective-permute-start.7 = (f32[4,2,32,1024]{3,2,1,0:T(8,128)S(1)}, f32[4,2,32,1024]{3,2,1,0:T(8,128)}, u32[]{:S(2)}, u32[]{:S(2)}) collective-permute-start(f32[4,2,32,1024]{3,2,1,0:T(8,128)S(1)} %get-tuple-element.170), channel_id=1, source_target_pairs={{0,4},{1,5},{2,6},{3,7},{4,8},{5,9},{6,10},{7,11},{8,12},{9,13},{1... | collective-permute-start | bytes 3145736 | tf_op jit(solution)/shard_map/ppermute | solution.py:14
Sparse Core Ops, SparseCore 0:
  299.6 147.1 all-reduce.12
where the time goes:
time: 465 us; the launch traced here: 460 us
  waiting for transfers between devices  191 us (41%)
  matrix products  118 us (25%)
  local copies, waits for them, and re-layouts  78.8 us (17%)
  other arithmetic  21.3 us (5%)
  starting transfers between devices  19.4 us (4%)
  loops' own time  15.7 us (3%)
  between operations  15.3 us (3%)
    psum x1, waiting for transfers between devices, on_device(): probe_grad = lax.psum(jnp.sum(probe_terms, axis=0), 'tile')  147 us
    dot_general x56, matrix products, product(): jnp.einsum('jk,mkl->mjl', matrix, field, precision=lax.Precision.HIGHEST)  62.5 us
    dot_general x56, matrix products, product(): jnp.einsum('mjk,kl->mjl', field, matrix, precision=lax.Precision.HIGHEST)  55.6 us
    ppermute x8, waiting for transfers between devices, from_behind(): return lax.ppermute(value, axis, pairs)  43.8 us
    dynamic_update_slice x4, local copies, waits for them, and re-layouts, add_window(): lax.dynamic_update_slice(gradient_buffer, current + crop_grads[window_ind...  28.6 us
    ppermute x8, starting transfers between devices, from_behind(): return lax.ppermute(value, axis, pairs)  19.4 us
    gather x12, local copies, waits for them, and re-layouts  17.1 us
    another operation x1, loops' own time, on_device(): lax.fori_loop(0, row_offset.shape[0], add_window, jnp.zeros(extended.shap...  15.6 us
  transfers between devices with their start and end apart: 9, of which 5 were waited for; matrix products, arithmetic and copies ran while one was open for 2% of the time, Pallas kernels for 0%

commit v1 on v0

--- a/solution.py
+++ b/solution.py
@@ -137,7 +137,7 @@
     own_grad = shares[0]
     for offset in range(1, upper_count + 1):
         own_grad = own_grad + from_behind(shares[offset], "tile", offset)
-    probe_grad = lax.psum(jnp.sum(probe_terms, axis=0), "tile")
+    probe_grad = jnp.sum(lax.all_gather(jnp.sum(probe_terms, axis=0), "tile"), axis=0)
     return (own_grad, probe_grad)
 
 

time: 465 us -> 395 us (0.85)
  the two profiles are of different devices: /device:TPU:0 before, /device:TPU:5 now
where the time goes in v1:
time: 395 us; the launch traced here: 390 us
  waiting for transfers between devices  142 us (36%)
  matrix products  117 us (30%)
  local copies, waits for them, and re-layouts  75.4 us (19%)
  other arithmetic  21.4 us (5%)
  loops' own time  15.7 us (4%)
  between operations  15.3 us (4%)
    ppermute x8, waiting for transfers between devices, from_behind(): return lax.ppermute(value, axis, pairs)  142 us
    dot_general x56, matrix products, product(): jnp.einsum('jk,mkl->mjl', matrix, field, precision=lax.Precision.HIGHEST)  61.5 us
    dot_general x56, matrix products, product(): jnp.einsum('mjk,kl->mjl', field, matrix, precision=lax.Precision.HIGHEST)  55.6 us
    dynamic_update_slice x4, local copies, waits for them, and re-layouts, add_window(): lax.dynamic_update_slice(gradient_buffer, current + crop_grads[window_ind...  28.6 us
    gather x12, local copies, waits for them, and re-layouts  16.2 us
    another operation x1, loops' own time, on_device(): lax.fori_loop(0, row_offset.shape[0], add_window, jnp.zeros(extended.shap...  15.6 us
  transfers between devices with their start and end apart: 9, of which 8 were waited for; matrix products, arithmetic and copies ran while one was open for 18% of the time, Pallas kernels for 0%

profile of v1, /device:TPU:5, one launch (start us, length us, event | category | flops | bytes accessed | tf_op | source)
XLA Modules:
  0.0 390.3 jit_solution(15213727466732788741)
XLA Ops:
  7.9 14.7 %collective-permute-done = f32[4,2,32,1024]{3,2,1,0:T(8,128)S(1)} collective-permute-done((f32[4,2,32,1024]{3,2,1,0:T(8,128)}, f32[4,2,32,1024]{3,2,1,0:T(8,128)S(1)}, u32[]{:S(2)}, u32[]{:S(2)}) %collective-permute-start) | collective-permute-done | bytes 1048608 | tf_op jit(solution)/shard_map/ppermute | solution.py:14
  22.6 15.1 %collective-permute-done.1 = f32[4,2,32,1024]{3,2,1,0:T(8,128)S(1)} collective-permute-done((f32[4,2,32,1024]{3,2,1,0:T(8,128)S(1)}, f32[4,2,32,1024]{3,2,1,0:T(8,128)S(1)}, u32[]{:S(2)}, u32[]{:S(2)}) %collective-permute-start.1) | collective-permute-done | bytes 1048608 | tf_op jit(solution)/shard_map/ppermute | solution.py:14
  40.0 12.8 %collective-permute-done.2 = f32[4,2,32,1024]{3,2,1,0:T(8,128)S(1)} collective-permute-done((f32[4,2,32,1024]{3,2,1,0:T(8,128)S(1)}, f32[4,2,32,1024]{3,2,1,0:T(8,128)S(1)}, u32[]{:S(2)}, u32[]{:S(2)}) %collective-permute-start.2) | collective-permute-done | bytes 1048608 | tf_op jit(solution)/shard_map/ppermute | solution.py:14
  53.8 1.3 constant_dynamic-update-slice_fusion.4
  56.4 11.7 %collective-permute-done.3 = f32[4,2,32,1024]{3,2,1,0:T(8,128)} collective-permute-done((f32[4,2,32,1024]{3,2,1,0:T(8,128)S(1)}, f32[4,2,32,1024]{3,2,1,0:T(8,128)}, u32[]{:S(2)}, u32[]{:S(2)}) %collective-permute-start.3) | collective-permute-done | bytes 1048608 | tf_op jit(solution)/shard_map/ppermute | solution.py:14
  68.1 1.3 constant_dynamic-update-slice_fusion
  69.5 3.2 pad_maximum_fusion
  72.6 16.4 %while.16 = (s32[]{:T(128)}, f32[4,2,159,1151]{3,2,1,0:T(8,128)}, s32[4,4]{1,0:T(4,128)S(1)}, f32[4,4,2,128,128]{4,3,2,1,0:T(8,128)}, s32[]{:T(128)}) while((s32[]{:T(128)}, f32[4,2,159,1151]{3,2,1,0:T(8,128)}, s32[4,4]{1,0:T(4,128)S(1)}, f32[4,4,2,128,128]{4,3,2,1,0:T(8,128)}, s32[]{:T(128)}) %tuple.90), condition=%wide.while_cond.1, body=%wide.while_body.1.sunk | while | flops 2 | bytes 1050225 | solution.py:113
  73.2 3.5 bitcast_dynamic-update-slice_fusion.2
  77.3 3.5 bitcast_dynamic-update-slice_fusion.2
  81.4 3.5 bitcast_dynamic-update-slice_fusion.2
  85.4 3.5 bitcast_dynamic-update-slice_fusion.2
  89.0 1.7 slice_bitcast_fusion.7
  98.9 1.2 fusion.84
  100.1 1.2 fusion.83
  101.3 1.4 fusion.38
  103.9 1.2 fusion.39
  108.5 1.2 fusion.236
  109.7 1.2 fusion.232
  110.9 1.2 fusion.37
  113.2 1.6 fusion.36
  118.2 1.2 fusion.86
  119.5 1.2 fusion.85
  120.7 1.2 fusion.34
  123.0 1.2 fusion.35
  125.4 1.3 convolution_add_fusion.34
  127.9 1.2 fusion.222
  129.1 1.2 fusion.218
  130.2 1.2 fusion.33
  132.6 1.2 fusion.32
  137.2 1.4 fusion.88
  138.6 1.2 fusion.87
  139.8 1.2 fusion.30
  142.2 1.2 fusion.31
  146.8 1.2 fusion.208
  148.0 1.2 fusion.204
  149.2 1.6 fusion.29
  150.9 1.2 fusion.28
  176.9 1.8 multiply_reduce_fusion.10
  187.1 1.3 fusion.11
  191.9 2.0 multiply_reduce_fusion.6
  207.6 1.3 add_bitcast_fusion.1
  215.9 3.0 broadcast_in_dim.12
  218.9 54.8 %while.15 = (s32[]{:T(128)}, f32[4,2,159,1151]{3,2,1,0:T(8,128)}, s32[4]{0:T(128)S(1)}, s32[4]{0:T(128)S(1)}, f32[4,4,2,128,128]{4,3,0,2,1:T(8,128)S(1)}, /*index=5*/s32[]{:T(128)}, s32[]{:T(128)}, s32[]{:T(128)}, s32[]{:T(128)}) while((s32[]{:T(128)}, f32[4,2,159,1151]{3,2,1,0:T(8,128)}, s32[4]{0:T(128)S(1)}, s32[4]{0:T(128)S(1)}, ...), condition=%wide.region_18.19_spmd, body=%wide.region_17.18_spmd.sunk | while | flops 131080 | bytes 2621641 | solution.py:123
  223.9 1.5 bitcast_add_fusion.2
  225.4 7.3 %dynamic_update_slice.8 = f32[4,2,159,1151]{3,2,1,0:T(8,128)} dynamic-update-slice(f32[4,2,159,1151]{3,2,1,0:T(8,128)} %get-tuple-element.285, f32[4,2,128,128]{3,2,1,0:T(8,128)S(1)} %bitcast_add_fusion.2, s32[]{:T(128)} %constant.98.clone.1..sunk, s32[]{:T(128)} %constant.98.clone.1..sunk, s32[]{:T(128)S(6)} %select_n.692, s32[]{:T(128)S(6)} %select_n.693) | dynamic-update-slice | bytes 1048580 | tf_op jit(solution)/shard_map/while/body/eval_jaxpr/dynamic_update_slice | solution.py:121
  237.9 1.5 bitcast_add_fusion.2
  239.3 7.0 %dynamic_update_slice.8 = f32[4,2,159,1151]{3,2,1,0:T(8,128)} dynamic-update-slice(f32[4,2,159,1151]{3,2,1,0:T(8,128)} %get-tuple-element.285, f32[4,2,128,128]{3,2,1,0:T(8,128)S(1)} %bitcast_add_fusion.2, s32[]{:T(128)} %constant.98.clone.1..sunk, s32[]{:T(128)} %constant.98.clone.1..sunk, s32[]{:T(128)S(6)} %select_n.692, s32[]{:T(128)S(6)} %select_n.693) | dynamic-update-slice | bytes 1048580 | tf_op jit(solution)/shard_map/while/body/eval_jaxpr/dynamic_update_slice | solution.py:121
  251.4 1.5 bitcast_add_fusion.2
  253.0 7.2 %dynamic_update_slice.8 = f32[4,2,159,1151]{3,2,1,0:T(8,128)} dynamic-update-slice(f32[4,2,159,1151]{3,2,1,0:T(8,128)} %get-tuple-element.285, f32[4,2,128,128]{3,2,1,0:T(8,128)S(1)} %bitcast_add_fusion.2, s32[]{:T(128)} %constant.98.clone.1..sunk, s32[]{:T(128)} %constant.98.clone.1..sunk, s32[]{:T(128)S(6)} %select_n.692, s32[]{:T(128)S(6)} %select_n.693) | dynamic-update-slice | bytes 1048580 | tf_op jit(solution)/shard_map/while/body/eval_jaxpr/dynamic_update_slice | solution.py:121
  265.2 1.5 bitcast_add_fusion.2
  266.7 7.0 %dynamic_update_slice.8 = f32[4,2,159,1151]{3,2,1,0:T(8,128)} dynamic-update-slice(f32[4,2,159,1151]{3,2,1,0:T(8,128)} %get-tuple-element.285, f32[4,2,128,128]{3,2,1,0:T(8,128)S(1)} %bitcast_add_fusion.2, s32[]{:T(128)} %constant.98.clone.1..sunk, s32[]{:T(128)} %constant.98.clone.1..sunk, s32[]{:T(128)S(6)} %select_n.692, s32[]{:T(128)S(6)} %select_n.693) | dynamic-update-slice | bytes 1048580 | tf_op jit(solution)/shard_map/while/body/eval_jaxpr/dynamic_update_slice | solution.py:121
  273.7 5.7 %slice.104 = f32[4,2,159,1024]{3,2,1,0:T(8,128)} slice(f32[4,2,159,1151]{3,2,1,0:T(8,128)} %get-tuple-element.108), slice={[0:4], [0:2], [0:159], [0:1024]} | slice | bytes 10420224 | tf_op jit(solution)/shard_map/slice | solution.py:127
  279.5 1.4 slice_add_fusion.1
  280.8 3.7 scatter-add.4
  284.5 2.5 fusion.846
  287.2 1.4 collective-permute-start.6
  288.6 1.5 collective-permute-start.7
  290.1 19.3 %collective-permute-done.4 = f32[4,2,32,1024]{3,2,1,0:T(8,128)S(1)} collective-permute-done((f32[4,2,32,1024]{3,2,1,0:T(8,128)S(1)}, f32[4,2,32,1024]{3,2,1,0:T(8,128)S(1)}, u32[]{:S(2)}, u32[]{:S(2)}) %collective-permute-start.4) | collective-permute-done | bytes 1048608 | tf_op jit(solution)/shard_map/ppermute | solution.py:14
  309.4 22.5 %collective-permute-done.5 = f32[4,2,32,1024]{3,2,1,0:T(8,128)S(1)} collective-permute-done((f32[4,2,32,1024]{3,2,1,0:T(8,128)S(1)}, f32[4,2,32,1024]{3,2,1,0:T(8,128)S(1)}, u32[]{:S(2)}, u32[]{:S(2)}) %collective-permute-start.5) | collective-permute-done | bytes 1048608 | tf_op jit(solution)/shard_map/ppermute | solution.py:14
  331.9 22.5 %collective-permute-done.6 = f32[4,2,32,1024]{3,2,1,0:T(8,128)S(1)} collective-permute-done((f32[4,2,32,1024]{3,2,1,0:T(8,128)S(1)}, f32[4,2,32,1024]{3,2,1,0:T(8,128)S(1)}, u32[]{:S(2)}, u32[]{:S(2)}) %collective-permute-start.6) | collective-permute-done | bytes 1048608 | tf_op jit(solution)/shard_map/ppermute | solution.py:14
  354.4 23.1 %collective-permute-done.7 = f32[4,2,32,1024]{3,2,1,0:T(8,128)S(1)} collective-permute-done((f32[4,2,32,1024]{3,2,1,0:T(8,128)S(1)}, f32[4,2,32,1024]{3,2,1,0:T(8,128)S(1)}, u32[]{:S(2)}, u32[]{:S(2)}) %collective-permute-start.7) | collective-permute-done | bytes 1048608 | tf_op jit(solution)/shard_map/ppermute | solution.py:14
  377.4 2.7 fusion.44
  380.2 3.1 reduce_sum.197
  (157 shorter events, 99.1 us)
Async XLA Ops:
  7.2 373.0 %all-gather.3.cloned.1.call-start = ((), (), s32[]{:S(2)}) async-start(), calls=%async_computation | async-start | bytes 4456448 | tf_op jit(solution)/shard_map/all_gather | solution.py:140
  7.2 15.4 %collective-permute-start = (f32[4,2,32,1024]{3,2,1,0:T(8,128)}, f32[4,2,32,1024]{3,2,1,0:T(8,128)S(1)}, u32[]{:S(2)}, u32[]{:S(2)}) collective-permute-start(f32[4,2,32,1024]{3,2,1,0:T(8,128)} %param.9), channel_id=1, source_target_pairs={{0,15},{1,0},{2,1},{3,2},{4,3},{5,4},{6,5},{7,6},{8,7},{9,8},{10,9... | collective-permute-start | bytes 3145736 | tf_op jit(solution)/shard_map/ppermute | solution.py:14
  22.6 15.1 %collective-permute-start.1 = (f32[4,2,32,1024]{3,2,1,0:T(8,128)S(1)}, f32[4,2,32,1024]{3,2,1,0:T(8,128)S(1)}, u32[]{:S(2)}, u32[]{:S(2)}) collective-permute-start(f32[4,2,32,1024]{3,2,1,0:T(8,128)S(1)} %collective-permute-done), channel_id=1, source_target_pairs={{0,15},{1,0},{2,1},{3,2},{4,3},{5,4},{6,5},{7,6},{8,7},{9,8},{10,9... | collective-permute-start | bytes 3145736 | tf_op jit(solution)/shard_map/ppermute | solution.py:14
  37.7 15.1 %collective-permute-start.2 = (f32[4,2,32,1024]{3,2,1,0:T(8,128)S(1)}, f32[4,2,32,1024]{3,2,1,0:T(8,128)S(1)}, u32[]{:S(2)}, u32[]{:S(2)}) collective-permute-start(f32[4,2,32,1024]{3,2,1,0:T(8,128)S(1)} %collective-permute-done.1), channel_id=1, source_target_pairs={{0,15},{1,0},{2,1},{3,2},{4,3},{5,4},{6,5},{7,6},{8,7},{9,8},{10,9... | collective-permute-start | bytes 3145736 | tf_op jit(solution)/shard_map/ppermute | solution.py:14
  52.8 15.2 %collective-permute-start.3 = (f32[4,2,32,1024]{3,2,1,0:T(8,128)S(1)}, f32[4,2,32,1024]{3,2,1,0:T(8,128)}, u32[]{:S(2)}, u32[]{:S(2)}) collective-permute-start(f32[4,2,32,1024]{3,2,1,0:T(8,128)S(1)} %collective-permute-done.2), channel_id=1, source_target_pairs={{0,15},{1,0},{2,1},{3,2},{4,3},{5,4},{6,5},{7,6},{8,7},{9,8},{10,9... | collective-permute-start | bytes 3145736 | tf_op jit(solution)/shard_map/ppermute | solution.py:14
  149.2 7.4 %copy-start.6 = (f32[4,128,128]{2,1,0:T(8,128)S(1)}, f32[4,128,128]{2,1,0:T(8,128)}, u32[]{:S(2)}) copy-start(f32[4,128,128]{2,1,0:T(8,128)} %param.13) | copy-start | bytes 786436
  208.9 4.4 %copy-start = (f32[4,128,128]{2,1,0:T(8,128)S(1)}, f32[4,128,128]{2,1,0:T(8,128)}, u32[]{:S(2)}) copy-start(f32[4,128,128]{2,1,0:T(8,128)} %get-tuple-element.133) | copy-start | bytes 786436
  208.9 4.4 %copy-start.1 = (f32[4,128,128]{2,1,0:T(8,128)S(1)}, f32[4,128,128]{2,1,0:T(8,128)}, u32[]{:S(2)}) copy-start(f32[4,128,128]{2,1,0:T(8,128)} %get-tuple-element.134) | copy-start | bytes 786436
  209.9 3.6 copy-start.2
  210.7 3.9 copy-start.3
  211.6 3.0 copy-start.4
  212.4 2.2 copy-start.5
  215.6 3.2 copy-start.7
  215.7 3.2 copy-start.8
  287.1 22.3 %collective-permute-start.4 = (f32[4,2,32,1024]{3,2,1,0:T(8,128)S(1)}, f32[4,2,32,1024]{3,2,1,0:T(8,128)S(1)}, u32[]{:S(2)}, u32[]{:S(2)}) collective-permute-start(f32[4,2,32,1024]{3,2,1,0:T(8,128)S(1)} %get-tuple-element.165), channel_id=1, source_target_pairs={{0,1},{1,2},{2,3},{3,4},{4,5},{5,6},{6,7},{7,8},{8,9},{9,10},{10,1... | collective-permute-start | bytes 3145736 | tf_op jit(solution)/shard_map/ppermute | solution.py:14
  287.1 44.8 %collective-permute-start.5 = (f32[4,2,32,1024]{3,2,1,0:T(8,128)S(1)}, f32[4,2,32,1024]{3,2,1,0:T(8,128)S(1)}, u32[]{:S(2)}, u32[]{:S(2)}) collective-permute-start(f32[4,2,32,1024]{3,2,1,0:T(8,128)S(1)} %get-tuple-element.168), channel_id=1, source_target_pairs={{0,2},{1,3},{2,4},{3,5},{4,6},{5,7},{6,8},{7,9},{8,10},{9,11},{10,... | collective-permute-start | bytes 3145736 | tf_op jit(solution)/shard_map/ppermute | solution.py:14
  287.2 67.2 %collective-permute-start.6 = (f32[4,2,32,1024]{3,2,1,0:T(8,128)S(1)}, f32[4,2,32,1024]{3,2,1,0:T(8,128)S(1)}, u32[]{:S(2)}, u32[]{:S(2)}) collective-permute-start(f32[4,2,32,1024]{3,2,1,0:T(8,128)S(1)} %get-tuple-element.167), channel_id=1, source_target_pairs={{0,3},{1,4},{2,5},{3,6},{4,7},{5,8},{6,9},{7,10},{8,11},{9,12},{10... | collective-permute-start | bytes 3145736 | tf_op jit(solution)/shard_map/ppermute | solution.py:14
  288.6 88.8 %collective-permute-start.7 = (f32[4,2,32,1024]{3,2,1,0:T(8,128)S(1)}, f32[4,2,32,1024]{3,2,1,0:T(8,128)S(1)}, u32[]{:S(2)}, u32[]{:S(2)}) collective-permute-start(f32[4,2,32,1024]{3,2,1,0:T(8,128)S(1)} %get-tuple-element.166), channel_id=1, source_target_pairs={{0,4},{1,5},{2,6},{3,7},{4,8},{5,9},{6,10},{7,11},{8,12},{9,13},{1... | collective-permute-start | bytes 3145736 | tf_op jit(solution)/shard_map/ppermute | solution.py:14
Sparse Core Ops, SparseCore 0:
  210.0 57.7 all-gather.2
